TPU v7x, 32 devices: a whole 2x2x4 slice. The times are simulated.
32 devices in a mesh: fsdp: 8 (over y, x, core), sp: 4 (over z).
Axes of the slice: x: 2, y: 2, z: 4, core: 2. Of those that a mesh axis runs over, the one named last changes fastest.
Arguments:
- hidden_in: bfloat16 [8, 1024, 2048], P('fsdp', 'sp'), may hold values from -6 to 6
- segments: int32 [8, 1024], P('fsdp'), may hold values from 0 to 3, never falling along the last dimension, each value on 1 to 640 neighbouring positions
- ln1_gain: float32 [2048], replicated, may hold values from 0.5 to 1.5
- ln1_bias: float32 [2048], replicated, may hold values from -1 to 1
- ln2_gain: float32 [2048], replicated, may hold values from 0.5 to 1.5
- ln2_bias: float32 [2048], replicated, may hold values from -1 to 1
- w_qkv: bfloat16 [6144, 2048], P('fsdp'), may hold values from -0.125 to 0.125
- b_qkv: float32 [6144], replicated, may hold values from -1 to 1
- w_dense: bfloat16 [2048, 2048], P('fsdp'), may hold values from -0.75 to 0.75
- b_dense: float32 [2048], replicated, may hold values from -1 to 1
- w_up: bfloat16 [8192, 2048], P('fsdp'), may hold values from -0.125 to 0.125
- b_up: float32 [8192], replicated, may hold values from -1 to 1
- w_down: bfloat16 [8192, 2048], P('fsdp'), may hold values from -0.0625 to 0.0625
- b_down: float32 [2048], replicated, may hold values from -1 to 1
- cotangent: bfloat16 [8, 1024, 2048], P('fsdp', 'sp'), may hold values from -6 to 6
Outputs:
- output: bfloat16 [8, 1024, 2048], P('fsdp', 'sp')
- input_grad: bfloat16 [8, 1024, 2048], P('fsdp', 'sp')
- grad_ln1_gain: float32 [2048], P('fsdp')
- grad_ln1_bias: float32 [2048], P('fsdp')
- grad_ln2_gain: float32 [2048], P('fsdp')
- grad_ln2_bias: float32 [2048], P('fsdp')
- grad_w_qkv: float32 [6144, 2048], P('fsdp')
- grad_b_qkv: float32 [6144], P('fsdp')
- grad_w_dense: float32 [2048, 2048], P('fsdp')
- grad_b_dense: float32 [2048], P('fsdp')
- grad_w_up: float32 [8192, 2048], P('fsdp')
- grad_b_up: float32 [8192], P('fsdp')
- grad_w_down: float32 [8192, 2048], P('fsdp')
- grad_b_down: float32 [2048], P('fsdp')
Inputs may be any that keep to these rules, and one draw needn't show every extreme that they name: `segments`: along each sequence the segment numbers never fall; each document is one run of 1 to 640 positions, and some document has exactly 640.
All inputs are finite; a program needn't handle non-finite values.
Results may differ from a plain program's by a relative error of at most 0.011.
Values may be sent and summed in bfloat16 or wider, within the bound.
A program may use at most 704 MiB of HBM per device.

v0:
```python
import math
import jax
import jax.numpy as jnp
from jax import lax
from jax.sharding import PartitionSpec as P

HEADS = 8
HEAD_DIM = 256
ROT = 64
EPSILON = 1e-05
NEGATIVE = -1e30
ROOT_HALF = 0.7071067811865476
ROOT_TWO_PI = 2.5066282746310002
SCALE = 1.0 / math.sqrt(HEAD_DIM)


def rounded(array):
    return lax.reduce_precision(array.astype(jnp.float32), 8, 7).astype(jnp.bfloat16)


def contract_rows(former, latter):
    return lax.dot_general(
        former, latter, (((0,), (0,)), ((), ())), preferred_element_type=jnp.float32
    )


def times_transposed(former, latter):
    return lax.dot_general(
        former, latter, (((1,), (1,)), ((), ())), preferred_element_type=jnp.float32
    )


def times(former, latter):
    return jnp.dot(former, latter, preferred_element_type=jnp.float32)


def norm_scaled(inputs):
    average = jnp.mean(inputs, axis=-1, keepdims=True)
    centred = inputs - average
    variance = jnp.mean(centred * centred, axis=-1, keepdims=True)
    inverse = lax.rsqrt(variance + EPSILON)
    return (centred * inverse, inverse)


def gelu_pair(hidden):
    cumulative = 0.5 * (1.0 + jax.scipy.special.erf(hidden * ROOT_HALF))
    return (
        hidden * cumulative,
        cumulative + hidden * jnp.exp(-0.5 * hidden * hidden) / ROOT_TWO_PI,
    )


def rotary_tables(segment_rows):
    length = segment_rows.shape[-1]
    places = jnp.arange(length, dtype=jnp.int32)
    changes = jnp.concatenate(
        [
            jnp.ones_like(segment_rows[..., :1]),
            (segment_rows[..., 1:] != segment_rows[..., :-1]).astype(jnp.int32),
        ],
        axis=-1,
    )
    first_place = lax.cummax(changes * places, axis=segment_rows.ndim - 1)
    position = (places - first_place).astype(jnp.float32)
    exponent = jnp.arange(0, ROT, 2).astype(jnp.float32) / ROT
    frequency = 1.0 / jnp.power(10000.0, exponent)
    angles = position[..., None] * frequency
    angles = jnp.concatenate([angles, angles], axis=-1)
    return (jnp.cos(angles), jnp.sin(angles))


def rotate(heads_part, cos_table, sin_table):
    half_rot = ROT // 2
    turned = heads_part[..., :ROT]
    swapped = jnp.concatenate([-turned[..., half_rot:], turned[..., :half_rot]], axis=-1)
    turned = turned * cos_table[..., None, :] + swapped * sin_table[..., None, :]
    return jnp.concatenate([turned, heads_part[..., ROT:]], axis=-1)


def unrotate(grads_part, cos_table, sin_table):
    half_rot = ROT // 2
    turned = grads_part[..., :ROT]
    along_sin = turned * sin_table[..., None, :]
    back_turn = jnp.concatenate([along_sin[..., half_rot:], -along_sin[..., :half_rot]], axis=-1)
    turned = turned * cos_table[..., None, :] + back_turn
    return jnp.concatenate([turned, grads_part[..., ROT:]], axis=-1)


def build_mask(segment_rows):
    places = jnp.arange(segment_rows.shape[-1], dtype=jnp.int32)
    return (segment_rows[:, :, None] == segment_rows[:, None, :]) & (
        places[None, :] <= places[:, None]
    )


def attention_scores(queries, keys_rot):
    return (
        jnp.einsum("bqhd,bkhd->bhqk", queries, keys_rot, preferred_element_type=jnp.float32) * SCALE
    )


def attend_forward(queries, keys_rot, values, mask):
    scores = jnp.where(mask[:, None], attention_scores(queries, keys_rot), NEGATIVE)
    row_top = jnp.max(scores, axis=-1, keepdims=True)
    exponent = jnp.exp(scores - row_top)
    row_total = jnp.sum(exponent, axis=-1, keepdims=True)
    attention = (exponent / row_total).astype(jnp.bfloat16)
    context = jnp.einsum("bhqk,bkhd->bqhd", attention, values, preferred_element_type=jnp.float32)
    return (context.astype(jnp.bfloat16), row_top + jnp.log(row_total))


def attend_backward(queries, keys_rot, values, mask, log_total, context_grad):
    scores = attention_scores(queries, keys_rot)
    attention = jnp.where(mask[:, None], jnp.exp(scores - log_total), 0.0)
    value_grad = jnp.einsum(
        "bhqk,bqhd->bkhd",
        attention.astype(jnp.bfloat16),
        context_grad,
        preferred_element_type=jnp.float32,
    )
    attention_grad = jnp.einsum(
        "bqhd,bkhd->bhqk", context_grad, values, preferred_element_type=jnp.float32
    )
    row_centre = jnp.sum(attention * attention_grad, axis=-1, keepdims=True)
    score_grad = (attention * (attention_grad - row_centre)).astype(jnp.bfloat16)
    query_grad = (
        jnp.einsum("bhqk,bkhd->bqhd", score_grad, keys_rot, preferred_element_type=jnp.float32)
        * SCALE
    )
    key_grad = (
        jnp.einsum("bhqk,bqhd->bkhd", score_grad, queries, preferred_element_type=jnp.float32)
        * SCALE
    )
    return (query_grad, key_grad, value_grad)


def sum_over_line(partial):
    inward = lax.ppermute(partial, "sp", [(0, 1), (3, 2)])
    half = rounded(partial.astype(jnp.float32) + inward.astype(jnp.float32))
    other = lax.ppermute(half, "sp", [(1, 2), (2, 1)])
    whole = rounded(half.astype(jnp.float32) + other.astype(jnp.float32))
    outward = lax.ppermute(whole, "sp", [(1, 0), (2, 3)])
    place = lax.axis_index("sp")
    inner = (place == 1) | (place == 2)
    return jnp.where(inner, whole, outward).astype(jnp.float32)


def sum_over_sp(partial):
    partial = rounded(partial)
    if lax.axis_size("sp") == 4:
        return sum_over_line(partial)
    return lax.psum(partial, "sp").astype(jnp.float32)


def per_device(
    hidden_in,
    segments,
    ln1_gain,
    ln1_bias,
    ln2_gain,
    ln2_bias,
    w_qkv,
    b_qkv,
    w_dense,
    b_dense,
    w_up,
    b_up,
    w_down,
    b_down,
    cotangent,
):
    seq_local, shard_len, width = hidden_in.shape
    seq_len = segments.shape[1]
    nf, ns = (lax.axis_size("fsdp"), lax.axis_size("sp"))
    f_place, s_place = (lax.axis_index("fsdp"), lax.axis_index("sp"))
    seqs = seq_local * nf
    group = seqs // ns
    piece = shard_len // nf
    tokens = group * seq_len
    per_head = max(1, nf // HEADS)
    head_count = max(1, HEADS // nf)
    head_sets = [[head * per_head + k for k in range(per_head)] for head in range(nf // per_head)]

    def gather_tokens(block):
        part = lax.all_to_all(block, "fsdp", split_axis=1, concat_axis=0, tiled=True)
        part = lax.all_to_all(part, "sp", split_axis=0, concat_axis=1, tiled=True)
        return lax.all_gather(part, "fsdp", axis=0, tiled=True).reshape(tokens, width)

    def scatter_tokens(partial):
        part = partial.reshape(nf * group, ns * piece, width)
        part = lax.psum_scatter(part, "fsdp", scatter_dimension=0, tiled=True)
        part = lax.all_to_all(part, "sp", split_axis=1, concat_axis=0, tiled=True)
        return lax.all_to_all(part, "fsdp", split_axis=0, concat_axis=1, tiled=True)

    def in_order(array):
        array = array.reshape(nf, group, ns, piece, -1)
        return array.transpose(1, 2, 0, 3, 4).reshape(group, seq_len, -1)

    def out_of_order(array):
        array = array.reshape(group, ns, nf, piece, -1)
        return array.transpose(2, 0, 1, 3, 4).reshape(tokens, -1)

    def over_head(array, axis):
        if per_head == 1:
            return array
        return lax.all_gather(array, "fsdp", axis=axis, tiled=True, axis_index_groups=head_sets)

    def own_columns(array):
        if per_head == 1:
            return array
        share = array.shape[-1] // per_head
        return lax.dynamic_slice_in_dim(array, f_place % per_head * share, share, array.ndim - 1)

    def own_part(vector):
        share = vector.shape[0] // nf
        return lax.dynamic_slice_in_dim(vector, f_place * share, share, 0)

    gathered = gather_tokens(hidden_in)
    upstream = gather_tokens(cotangent)
    rows = lax.all_gather(segments, "fsdp", axis=0, tiled=True)
    rows = lax.dynamic_slice_in_dim(rows, s_place * group, group, 0)
    dense_in = lax.all_to_all(w_dense, "fsdp", split_axis=1, concat_axis=0, tiled=True)
    head_qkv = over_head(w_qkv, 0)
    head_dense = over_head(dense_in, 1)
    head_bias = lax.dynamic_slice_in_dim(
        b_qkv, f_place // per_head * head_qkv.shape[0], head_qkv.shape[0], 0
    )
    scaled, _ = norm_scaled(gathered.astype(jnp.float32))
    normed = (scaled * ln1_gain + ln1_bias).astype(jnp.bfloat16)
    normed_mlp = (scaled * ln2_gain + ln2_bias).astype(jnp.bfloat16)
    hidden = times_transposed(normed_mlp, w_up) + own_part(b_up)
    activated, slope = gelu_pair(hidden)
    activated = activated.astype(jnp.bfloat16)
    hidden_grad = (times_transposed(upstream, w_down) * slope).astype(jnp.bfloat16)
    down_term = contract_rows(activated, upstream)
    up_term = contract_rows(hidden_grad, normed_mlp)
    mlp_norm_grad = times(hidden_grad, w_up)
    packed = (times_transposed(normed, head_qkv) + head_bias).astype(jnp.bfloat16)
    packed = in_order(packed).reshape(group, seq_len, head_count, 3 * HEAD_DIM)
    cos_table, sin_table = rotary_tables(rows)
    queries = rotate(packed[..., :HEAD_DIM].astype(jnp.float32), cos_table, sin_table).astype(
        jnp.bfloat16
    )
    keys_rot = rotate(
        packed[..., HEAD_DIM : 2 * HEAD_DIM].astype(jnp.float32), cos_table, sin_table
    ).astype(jnp.bfloat16)
    values = packed[..., 2 * HEAD_DIM :]
    mask = build_mask(rows)
    context, log_total = attend_forward(queries, keys_rot, values, mask)
    context = own_columns(out_of_order(context))
    partial_out = times_transposed(context, dense_in) + times(activated, w_down)
    context_grad = in_order(times(upstream, head_dense).astype(jnp.bfloat16)).reshape(
        group, seq_len, head_count, HEAD_DIM
    )
    query_grad, key_grad, value_grad = attend_backward(
        queries, keys_rot, values, mask, log_total, context_grad
    )
    packed_grad = jnp.concatenate(
        [
            unrotate(query_grad, cos_table, sin_table),
            unrotate(key_grad, cos_table, sin_table),
            value_grad,
        ],
        axis=-1,
    ).astype(jnp.bfloat16)
    packed_grad = own_columns(out_of_order(packed_grad))
    attn_norm_grad = times(packed_grad, w_qkv)
    qkv_term = contract_rows(packed_grad, normed)
    dense_term = contract_rows(upstream, context).astype(jnp.bfloat16)
    dense_term = lax.all_to_all(dense_term, "fsdp", split_axis=0, concat_axis=1, tiled=True)
    vectors = jnp.stack(
        [
            jnp.sum(attn_norm_grad * scaled, axis=0),
            jnp.sum(attn_norm_grad, axis=0),
            jnp.sum(mlp_norm_grad * scaled, axis=0),
            jnp.sum(mlp_norm_grad, axis=0),
        ],
        axis=1,
    )
    vectors = lax.psum_scatter(vectors, "fsdp", scatter_dimension=0, tiled=True)
    bias_out = own_part(jnp.sum(upstream.astype(jnp.float32), axis=0))
    bias_qkv = jnp.sum(packed_grad.astype(jnp.float32), axis=0)
    bias_up = jnp.sum(hidden_grad.astype(jnp.float32), axis=0)
    vectors, bias_out, bias_qkv, bias_up = lax.psum((vectors, bias_out, bias_qkv, bias_up), "sp")
    output = scatter_tokens(rounded(partial_out))
    weighted = scatter_tokens(rounded(attn_norm_grad * ln1_gain + mlp_norm_grad * ln2_gain))
    inputs = hidden_in.astype(jnp.float32)
    output = (inputs + (output.astype(jnp.float32) + (b_dense + b_down))).astype(jnp.bfloat16)
    own_scaled, own_inverse = norm_scaled(inputs)
    weighted = weighted.astype(jnp.float32)
    first_mean = jnp.mean(weighted, axis=-1, keepdims=True)
    second_mean = jnp.mean(weighted * own_scaled, axis=-1, keepdims=True)
    input_grad = (
        cotangent.astype(jnp.float32)
        + own_inverse * (weighted - first_mean - own_scaled * second_mean)
    ).astype(jnp.bfloat16)
    grad_down_w = sum_over_sp(down_term)
    grad_up_w = sum_over_sp(up_term)
    grad_qkv_w = sum_over_sp(qkv_term)
    grad_dense_w = sum_over_sp(dense_term)
    return (
        output,
        input_grad,
        vectors[:, 0],
        vectors[:, 1],
        vectors[:, 2],
        vectors[:, 3],
        grad_qkv_w,
        bias_qkv,
        grad_dense_w,
        bias_out,
        grad_up_w,
        bias_up,
        grad_down_w,
        bias_out,
    )


def solution(mesh):
    rows = P("fsdp", "sp", None)
    first = P("fsdp", None)
    return jax.shard_map(
        per_device,
        mesh=mesh,
        in_specs=(
            rows,
            first,
            P(),
            P(),
            P(),
            P(),
            first,
            P(),
            first,
            P(),
            first,
            P(),
            first,
            P(),
            rows,
        ),
        out_specs=(
            rows,
            rows,
            P("fsdp"),
            P("fsdp"),
            P("fsdp"),
            P("fsdp"),
            first,
            P("fsdp"),
            first,
            P("fsdp"),
            first,
            P("fsdp"),
            first,
            P("fsdp"),
        ),
        check_vma=False,
    )
```

profile of v0, /device:TPU:0, one launch (start us, length us, event | category | flops | bytes accessed | tf_op | source)
XLA Modules:
  0.0 1062.1 jit_solution(14219116837195556078)
XLA Ops:
  12.1 9.0 reduce.19
  23.7 20.6 %all_to_all.146 = bf16[8,2,32768]{2,1,0:T(2,128)(2,1)} all-to-all(bf16[8,2,32768]{2,1,0:T(2,128)(2,1)} %reshape.579), channel_id=1, replica_groups=mesh['fsdp'=8,'sp'=4] {'fsdp'}, dimensions={0} | all-to-all | bytes 2097152 | tf_op jit(solution)/shard_map/all_to_all | solution.py:185
  52.3 30.2 %all_to_all.147 = bf16[8,32,2048]{2,1,0:T(8,128)(2,1)S(1)} all-to-all(bf16[8,32,2048]{2,1,0:T(8,128)(2,1)S(1)} %bitcast.199), channel_id=1, replica_groups=mesh['fsdp'=8,'sp'=4] {'sp'}, dimensions={0} | all-to-all | bytes 2097152 | tf_op jit(solution)/shard_map/all_to_all | solution.py:186
  88.0 9.2 reduce.20
  99.8 26.8 %all_to_all.148 = bf16[8,2,32768]{2,1,0:T(2,128)(2,1)} all-to-all(bf16[8,2,32768]{2,1,0:T(2,128)(2,1)} %reshape.581), channel_id=1, replica_groups=mesh['fsdp'=8,'sp'=4] {'fsdp'}, dimensions={0} | all-to-all | bytes 2097152 | tf_op jit(solution)/shard_map/all_to_all | solution.py:185
  134.6 26.5 %all_to_all.149 = bf16[8,32,2048]{2,1,0:T(8,128)(2,1)S(1)} all-to-all(bf16[8,32,2048]{2,1,0:T(8,128)(2,1)S(1)} %bitcast.200), channel_id=1, replica_groups=mesh['fsdp'=8,'sp'=4] {'sp'}, dimensions={0} | all-to-all | bytes 2097152 | tf_op jit(solution)/shard_map/all_to_all | solution.py:186
  168.7 26.7 %all-gather = s32[8,1,1024]{2,1,0:T(1,128)S(1)} all-gather(s32[1,1,1024]{2,1,0:T(1,128)S(1)} %bitcast.233), channel_id=1, replica_groups=mesh['fsdp'=8,'sp'=4] {'fsdp'}, dimensions={0}, use_global_device_ids=true | all-gather | bytes 36864 | tf_op jit(solution)/shard_map/all_gather | solution.py:220
  298.7 15.7 %multiply_convert_fusion.1 = (bf16[2048,1024]{1,0:T(8,128)(2,1)}, f32[2048,1024]{1,0:T(8,128)}) fusion(f32[1024]{0:T(1024)S(1)} %dynamic_slice.14, bf16[2048,2048]{1,0:T(8,128)(2,1)} %get-tuple-element.26, bf16[1024,2048]{1,0:T(8,128)(2,1)S(1)} %copy-done.39), kind=kOutput, calls=%fused_computation.29 | convolution fusion | flops 8602517504 | bytes 25169920 | tf_op jit(solution)/shard_map/dot_general | solution.py:28
  314.4 17.5 %convert_reduce_fusion.2 = (f32[1024]{0:T(1024)}, bf16[2048,1024]{1,0:T(8,128)(2,1)}) fusion(f32[2048,1024]{1,0:T(8,128)} %get-tuple-element.60, f32[1024]{0:T(1024)S(1)} %dynamic_slice.14, bf16[2048,2048]{1,0:T(8,128)(2,1)S(1)} %bitcast.176, bf16[1024,2048]{1,0:T(8,128)(2,1)} %param.27), kind=kOutput, calls=%fused_computation.22 | convolution fusion | flops 8617196544 | bytes 25174016 | tf_op jit(solution)/shard_map/dot_general | solution.py:28
  331.9 14.1 %fusion.59 = f32[2048,2048]{1,0:T(8,128)} fusion(bf16[2048,1024]{1,0:T(8,128)(2,1)} %get-tuple-element.62, bf16[1024,2048]{1,0:T(8,128)(2,1)S(1)} %copy-done.39), kind=kOutput, calls=%fused_computation.148 | convolution fusion | flops 8589934592 | bytes 25165824 | tf_op jit(solution)/shard_map/dot_general | solution.py:34
  346.0 17.8 %multiply_reduce_fusion.1 = (f32[2048]{0:T(1024)S(1)}, f32[2048]{0:T(1024)S(1)}, f32[2048]{0:T(1024)S(1)}, f32[2048]{0:T(1024)S(1)}, bf16[2048,2048]{1,0:T(8,128)(2,1)}) fusion(bf16[16,128,2048]{2,1,0:T(8,128)(2,1)} %all-gather.4.cloned.1.call-done, f32[2048]{0:T(1024)S(1)} %get-tuple-element.48, f32[2048]{0:T(1024)S(1)} %get-tuple-element.49, ...), kind=kOutput, calls=%fused_computation.5 | convolution fusion | flops 6501163008 | bytes 39911424 | tf_op jit(solution)/shard_map/dot_general | solution.py:34
  373.6 15.8 %reduce-precision_convert_fusion.7 = bf16[1024,2048]{1,0:T(8,128)(2,1)} fusion(bf16[2048,1024]{1,0:T(8,128)(2,1)} %get-tuple-element.62, bf16[2048,2048]{1,0:T(8,128)(2,1)} %get-tuple-element.26), kind=kOutput, calls=%fused_computation.25 | convolution fusion | flops 8594128896 | bytes 16777216 | tf_op jit(solution)/shard_map/dot_general | solution.py:22
  395.1 11.7 %fusion.58 = f32[2048,2048]{1,0:T(8,128)} fusion(bf16[2048,1024]{1,0:T(8,128)(2,1)S(1)} %copy-done.41, bf16[1024,2048]{1,0:T(8,128)(2,1)S(1)} %copy-done.40), kind=kOutput, calls=%fused_computation.147 | convolution fusion | flops 8589934592 | bytes 25165824 | tf_op jit(solution)/shard_map/dot_general | solution.py:34
  406.8 11.7 %reduce-precision_convert_fusion.1 = bf16[2048,2048]{1,0:T(8,128)(2,1)} fusion(f32[2048,2048]{1,0:T(8,128)} %fusion.58, bf16[2048,256]{1,0:T(8,128)(2,1)S(1)} %bitcast.188, bf16[2048,256]{1,0:T(8,128)(2,1)S(1)} %bitcast.212), kind=kOutput, calls=%fused_computation.7 | convolution fusion | flops 2160066560 | bytes 27262976 | tf_op jit(solution)/shard_map/dot_general | solution.py:28
  418.5 14.7 %reduce-precision_convert_fusion.4 = bf16[1024,2048]{1,0:T(8,128)(2,1)} fusion(bf16[2048,1024]{1,0:T(8,128)(2,1)} %get-tuple-element.59, bf16[2048,2048]{1,0:T(8,128)(2,1)} %bitcast.173), kind=kOutput, calls=%fused_computation.21 | convolution fusion | flops 8594128896 | bytes 16777216 | tf_op jit(solution)/shard_map/dot_general | solution.py:22
  442.8 8.3 reduce-precision_convert_fusion.10
  454.0 30.2 %collective-permute-done.6 = bf16[1024,2048]{1,0:T(8,128)(2,1)} collective-permute-done((bf16[1024,2048]{1,0:T(8,128)(2,1)}, bf16[1024,2048]{1,0:T(8,128)(2,1)}, u32[]{:S(2)}, u32[]{:S(2)}) %collective-permute-start.6) | collective-permute-done | bytes 4194336 | tf_op jit(solution)/shard_map/ppermute | solution.py:138
  484.3 7.9 reduce-precision_convert_fusion.6
  501.8 72.4 %collective-permute-done.9 = bf16[1024,2048]{1,0:T(8,128)(2,1)} collective-permute-done((bf16[1024,2048]{1,0:T(8,128)(2,1)}, bf16[1024,2048]{1,0:T(8,128)(2,1)}, u32[]{:S(2)}, u32[]{:S(2)}) %collective-permute-start.9) | collective-permute-done | bytes 4194336 | tf_op jit(solution)/shard_map/ppermute | solution.py:138
  584.6 56.3 %collective-permute-done = bf16[768,2048]{1,0:T(8,128)(2,1)} collective-permute-done((bf16[768,2048]{1,0:T(8,128)(2,1)}, bf16[768,2048]{1,0:T(8,128)(2,1)}, u32[]{:S(2)}, u32[]{:S(2)}) %collective-permute-start) | collective-permute-done | bytes 3145760 | tf_op jit(solution)/shard_map/ppermute | solution.py:138
  655.6 20.9 %collective-permute-done.3 = bf16[256,2048]{1,0:T(8,128)(2,1)S(1)} collective-permute-done((bf16[256,2048]{1,0:T(8,128)(2,1)S(1)}, bf16[256,2048]{1,0:T(8,128)(2,1)S(1)}, u32[]{:S(2)}, u32[]{:S(2)}) %collective-permute-start.3) | collective-permute-done | bytes 1048608 | tf_op jit(solution)/shard_map/ppermute | solution.py:138
  697.3 63.8 %all-to-all-start.7 = ((bf16[2,128,2048]{2,0,1:T(2,128)(2,1)}), bf16[2,128,2048]{2,0,1:T(2,128)(2,1)}, u32[]{:S(2)}, u32[]{:S(2)}) async-start(bf16[2,128,2048]{2,0,1:T(2,128)(2,1)} %copy.202), calls=%async_computation.9 | async-start | bytes 2097152 | tf_op jit(solution)/shard_map/all_to_all | solution.py:192
  777.8 89.9 %all-to-all-done.7 = bf16[2,128,2048]{2,0,1:T(2,128)(2,1)} async-done(((bf16[2,128,2048]{2,0,1:T(2,128)(2,1)}), bf16[2,128,2048]{2,0,1:T(2,128)(2,1)}, u32[]{:S(2)}, u32[]{:S(2)}) %all-to-all-start.7) | async-done | bytes 1048608 | tf_op jit(solution)/shard_map/all_to_all | solution.py:192
  878.6 126.6 %all-reduce.1 = (f32[256,4]{0,1:T(4,128)S(1)}, f32[768]{0:T(1024)}, f32[256]{0:T(256)S(1)}, f32[1024]{0:T(1024)}) all-reduce(f32[256,4]{0,1:T(4,128)S(1)} %copy.219, f32[768]{0:T(1024)S(1)} %convert_reduce_fusion.3, f32[256]{0:T(256)S(1)} %dynamic_slice.15, f32[1024]{0:T(1024)S(1)} %copy-done.37), channel_id=1, replica_groups=mesh['fsdp'=8,'sp'=4] {'sp'}, use_global_device_ids=true, to_apply=%region_18.19 | all-reduce | flops 3072 | bytes 24576 | tf_op jit(solution)/shard_map/psum | solution.py:284
  (242 shorter events, 302.8 us)
Async XLA Ops:
  7.2 212.3 %copy-start = (bf16[768,2048]{1,0:T(8,128)(2,1)S(1)}, bf16[768,2048]{1,0:T(8,128)(2,1)}, u32[]{:S(2)}) copy-start(bf16[768,2048]{1,0:T(8,128)(2,1)} %param.21) | copy-start | bytes 9437188
  7.2 195.9 %all-gather.4.cloned.1.call-start = ((), (), s32[]{:S(2)}) async-start(), calls=%async_computation.13 | async-start | bytes 9437184 | tf_op jit(solution)/shard_map/all_gather | solution.py:187
  83.5 147.9 %all-gather.6.cloned.1.call-start = ((), (), s32[]{:S(2)}) async-start(), calls=%async_computation.15 | async-start | bytes 9437184 | tf_op jit(solution)/shard_map/all_gather | solution.py:187
  164.4 36.5 %all-to-all-start.2 = ((bf16[256,8,256]{0,2,1:T(8,128)(2,1)}), bf16[256,8,256]{0,2,1:T(8,128)(2,1)}, u32[]{:S(2)}, u32[]{:S(2)}) async-start(bf16[256,8,256]{0,2,1:T(8,128)(2,1)} %bitcast.204), calls=%async_computation.2 | async-start | bytes 2097152 | tf_op jit(solution)/shard_map/all_to_all | solution.py:222
  168.7 525.4 %reduce-scatter.8.cloned.1.call-start = ((), (), s32[]{:S(2)}) async-start(), calls=%async_computation.16 | async-start | bytes 9437184 | tf_op jit(solution)/shard_map/reduce_scatter | solution.py:191
  363.8 410.5 %reduce-scatter.6.cloned.1.call-start = ((), (), s32[]{:S(2)}) async-start(), calls=%async_computation.14 | async-start | bytes 9437184 | tf_op jit(solution)/shard_map/reduce_scatter | solution.py:191
  389.4 94.8 %collective-permute-start.6 = (bf16[1024,2048]{1,0:T(8,128)(2,1)}, bf16[1024,2048]{1,0:T(8,128)(2,1)}, u32[]{:S(2)}, u32[]{:S(2)}) collective-permute-start(bf16[1024,2048]{1,0:T(8,128)(2,1)} %reduce-precision_convert_fusion.7), channel_id=1, source_target_pairs={{0,1},{3,2},{4,5},{7,6},{8,9},{11,10},{12,13},{15,14},{16,17},{19,... | collective-permute-start | bytes 12582920 | tf_op jit(solution)/shard_map/ppermute | solution.py:138
  433.2 140.9 %collective-permute-start.9 = (bf16[1024,2048]{1,0:T(8,128)(2,1)}, bf16[1024,2048]{1,0:T(8,128)(2,1)}, u32[]{:S(2)}, u32[]{:S(2)}) collective-permute-start(bf16[1024,2048]{1,0:T(8,128)(2,1)} %reduce-precision_convert_fusion.4), channel_id=1, source_target_pairs={{0,1},{3,2},{4,5},{7,6},{8,9},{11,10},{12,13},{15,14},{16,17},{19,... | collective-permute-start | bytes 12582920 | tf_op jit(solution)/shard_map/ppermute | solution.py:138
  451.1 189.8 %collective-permute-start = (bf16[768,2048]{1,0:T(8,128)(2,1)}, bf16[768,2048]{1,0:T(8,128)(2,1)}, u32[]{:S(2)}, u32[]{:S(2)}) collective-permute-start(bf16[768,2048]{1,0:T(8,128)(2,1)} %reduce-precision_convert_fusion.10), channel_id=1, source_target_pairs={{0,1},{3,2},{4,5},{7,6},{8,9},{11,10},{12,13},{15,14},{16,17},{19,... | collective-permute-start | bytes 9437192 | tf_op jit(solution)/shard_map/ppermute | solution.py:138
  492.1 185.5 %collective-permute-start.7 = (bf16[1024,2048]{1,0:T(8,128)(2,1)}, bf16[1024,2048]{1,0:T(8,128)(2,1)}, u32[]{:S(2)}, u32[]{:S(2)}) collective-permute-start(bf16[1024,2048]{1,0:T(8,128)(2,1)} %reduce-precision_convert_fusion.6), channel_id=1, source_target_pairs={{1,2},{2,1},{5,6},{6,5},{9,10},{10,9},{13,14},{14,13},{17,18},{18,... | collective-permute-start | bytes 12582920 | tf_op jit(solution)/shard_map/ppermute | solution.py:140
  498.2 151.1 %all-to-all-start.9 = ((bf16[8,256,256]{1,2,0:T(8,128)(2,1)}), bf16[8,256,256]{1,2,0:T(8,128)(2,1)S(1)}, u32[]{:S(2)}, u32[]{:S(2)}) async-start(bf16[8,256,256]{1,2,0:T(8,128)(2,1)} %bitcast.164), calls=%async_computation.11 | async-start | bytes 2097152 | tf_op jit(solution)/shard_map/all_to_all | solution.py:270
  581.8 179.4 %collective-permute-start.10 = (bf16[1024,2048]{1,0:T(8,128)(2,1)}, bf16[1024,2048]{1,0:T(8,128)(2,1)}, u32[]{:S(2)}, u32[]{:S(2)}) collective-permute-start(bf16[1024,2048]{1,0:T(8,128)(2,1)} %reduce-precision_convert_fusion.3), channel_id=1, source_target_pairs={{1,2},{2,1},{5,6},{6,5},{9,10},{10,9},{13,14},{14,13},{17,18},{18,... | collective-permute-start | bytes 12582920 | tf_op jit(solution)/shard_map/ppermute | solution.py:140
  647.0 39.6 %collective-permute-start.1 = (bf16[768,2048]{1,0:T(8,128)(2,1)}, bf16[768,2048]{1,0:T(8,128)(2,1)}, u32[]{:S(2)}, u32[]{:S(2)}) collective-permute-start(bf16[768,2048]{1,0:T(8,128)(2,1)} %reduce-precision_convert_fusion.9), channel_id=1, source_target_pairs={{1,2},{2,1},{5,6},{6,5},{9,10},{10,9},{13,14},{14,13},{17,18},{18,... | collective-permute-start | bytes 9437192 | tf_op jit(solution)/shard_map/ppermute | solution.py:140
  650.1 26.4 %collective-permute-start.3 = (bf16[256,2048]{1,0:T(8,128)(2,1)S(1)}, bf16[256,2048]{1,0:T(8,128)(2,1)S(1)}, u32[]{:S(2)}, u32[]{:S(2)}) collective-permute-start(bf16[256,2048]{1,0:T(8,128)(2,1)S(1)} %copy.206), channel_id=1, source_target_pairs={{0,1},{3,2},{4,5},{7,6},{8,9},{11,10},{12,13},{15,14},{16,17},{19,... | collective-permute-start | bytes 3145736 | tf_op jit(solution)/shard_map/ppermute | solution.py:138
  676.9 93.4 %collective-permute-start.4 = (bf16[256,2048]{1,0:T(8,128)(2,1)S(1)}, bf16[256,2048]{1,0:T(8,128)(2,1)S(1)}, u32[]{:S(2)}, u32[]{:S(2)}) collective-permute-start(bf16[256,2048]{1,0:T(8,128)(2,1)S(1)} %reduce-precision_convert_fusion.12), channel_id=1, source_target_pairs={{1,2},{2,1},{5,6},{6,5},{9,10},{10,9},{13,14},{14,13},{17,18},{18,... | collective-permute-start | bytes 3145736 | tf_op jit(solution)/shard_map/ppermute | solution.py:140
  685.3 334.4 %collective-permute-start.8 = (bf16[1024,2048]{1,0:T(8,128)(2,1)}, bf16[1024,2048]{1,0:T(8,128)(2,1)}, u32[]{:S(2)}, u32[]{:S(2)}) collective-permute-start(bf16[1024,2048]{1,0:T(8,128)(2,1)} %reduce-precision_convert_fusion.5), channel_id=1, source_target_pairs={{1,0},{2,3},{5,4},{6,7},{9,8},{10,11},{13,12},{14,15},{17,16},{18,... | collective-permute-start | bytes 12582920 | tf_op jit(solution)/shard_map/ppermute | solution.py:142
  692.7 322.0 %collective-permute-start.2 = (bf16[768,2048]{1,0:T(8,128)(2,1)}, bf16[768,2048]{1,0:T(8,128)(2,1)}, u32[]{:S(2)}, u32[]{:S(2)}) collective-permute-start(bf16[768,2048]{1,0:T(8,128)(2,1)} %reduce-precision_convert_fusion.8), channel_id=1, source_target_pairs={{1,0},{2,3},{5,4},{6,7},{9,8},{10,11},{13,12},{14,15},{17,16},{18,... | collective-permute-start | bytes 9437192 | tf_op jit(solution)/shard_map/ppermute | solution.py:142
  697.3 170.4 %all-to-all-start.7 = ((bf16[2,128,2048]{2,0,1:T(2,128)(2,1)}), bf16[2,128,2048]{2,0,1:T(2,128)(2,1)}, u32[]{:S(2)}, u32[]{:S(2)}) async-start(bf16[2,128,2048]{2,0,1:T(2,128)(2,1)} %copy.202), calls=%async_computation.9 | async-start | bytes 2097152 | tf_op jit(solution)/shard_map/all_to_all | solution.py:192
  761.1 116.5 %reduce-scatter.10.cloned.1.call-start = ((), (), s32[]{:S(2)}) async-start(), calls=%async_computation.17 | async-start | bytes 1179648
  768.9 265.4 %collective-permute-start.11 = (bf16[1024,2048]{1,0:T(8,128)(2,1)}, bf16[1024,2048]{1,0:T(8,128)(2,1)}, u32[]{:S(2)}, u32[]{:S(2)}) collective-permute-start(bf16[1024,2048]{1,0:T(8,128)(2,1)} %reduce-precision_convert_fusion.2), channel_id=1, source_target_pairs={{1,0},{2,3},{5,4},{6,7},{9,8},{10,11},{13,12},{14,15},{17,16},{18,... | collective-permute-start | bytes 12582920 | tf_op jit(solution)/shard_map/ppermute | solution.py:142
  771.6 234.2 %collective-permute-start.5 = (bf16[256,2048]{1,0:T(8,128)(2,1)}, bf16[256,2048]{1,0:T(8,128)(2,1)}, u32[]{:S(2)}, u32[]{:S(2)}) collective-permute-start(bf16[256,2048]{1,0:T(8,128)(2,1)} %reduce-precision_convert_fusion.11), channel_id=1, source_target_pairs={{1,0},{2,3},{5,4},{6,7},{9,8},{10,11},{13,12},{14,15},{17,16},{18,... | collective-permute-start | bytes 3145736 | tf_op jit(solution)/shard_map/ppermute | solution.py:142
  867.7 143.4 %all-to-all-start.3 = ((bf16[2,128,2048]{2,0,1:T(2,128)(2,1)}), bf16[2,128,2048]{2,0,1:T(2,128)(2,1)}, u32[]{:S(2)}, u32[]{:S(2)}) async-start(bf16[2,128,2048]{2,0,1:T(2,128)(2,1)} %copy.186), calls=%async_computation.4 | async-start | bytes 2097152 | tf_op jit(solution)/shard_map/all_to_all | solution.py:192
  1011.2 18.9 %all-to-all-start.8 = ((bf16[8,32,2048]{2,1,0:T(8,128)(2,1)}), bf16[8,32,2048]{2,1,0:T(8,128)(2,1)S(1)}, u32[]{:S(2)}, u32[]{:S(2)}) async-start(bf16[8,32,2048]{2,1,0:T(8,128)(2,1)} %bitcast.55), calls=%async_computation.10 | async-start | bytes 2097152 | tf_op jit(solution)/shard_map/all_to_all | solution.py:193
  1030.1 19.7 %all-to-all-start.4 = ((bf16[8,32,2048]{2,1,0:T(8,128)(2,1)}), bf16[8,32,2048]{2,1,0:T(8,128)(2,1)}, u32[]{:S(2)}, u32[]{:S(2)}) async-start(bf16[8,32,2048]{2,1,0:T(8,128)(2,1)} %bitcast.27), calls=%async_computation.5 | async-start | bytes 2097152 | tf_op jit(solution)/shard_map/all_to_all | solution.py:193
  (45 other events, 680.8 us)
Sparse Core Ops, SparseCore 0:
  83.7 59.1 all-gather.3
  162.2 62.2 all-gather.5
  364.0 71.4 reduce-scatter.7
  439.7 78.5 reduce-scatter.5
  774.4 44.9 reduce-scatter.9
where the time goes:
time: 1070 us; the launch traced here: 1060 us
  waiting for transfers between devices  276 us (26%)
  blocking collectives  257 us (24%)
  matrix products  168 us (16%)
  other arithmetic  151 us (14%)
  starting transfers between devices  115 us (11%)
  local copies, waits for them, and re-layouts  79.8 us (7%)
  between operations  15.1 us (1%)
    ppermute x4, waiting for transfers between devices, sum_over_line(): inward = lax.ppermute(partial, 'sp', [(0, 1), (3, 2)])  180 us
    psum x1, blocking collectives, per_device(): lax.psum((vectors, bias_out, bias_qkv, bias_up), 'sp')  127 us
    all_to_all x2, waiting for transfers between devices, scatter_tokens(): part = lax.all_to_all(part, 'sp', split_axis=1, concat_axis=0, tiled=True)  89.9 us
    all_to_all x2, starting transfers between devices, scatter_tokens(): part = lax.all_to_all(part, 'sp', split_axis=1, concat_axis=0, tiled=True)  68.4 us
    all_to_all x2, blocking collectives, gather_tokens(): part = lax.all_to_all(part, 'sp', split_axis=0, concat_axis=1, tiled=True)  56.6 us
    dot_general x4, matrix products, times_transposed(): lax.dot_general(former, latter, (((1,), (1,)), ((), ())), preferred_eleme...  52 us
    dot_general x4, matrix products, times(): return jnp.dot(former, latter, preferred_element_type=jnp.float32)  49.7 us
    all_to_all x2, blocking collectives, gather_tokens(): lax.all_to_all(block, 'fsdp', split_axis=1, concat_axis=0, tiled=True)  47.4 us
  transfers between devices with their start and end apart: 23, of which 7 were waited for; matrix products, arithmetic and copies ran while one was open for 22% of the time, Pallas kernels for 0%

commit v1 on v0

--- a/solution.py
+++ b/solution.py
@@ -182,7 +182,12 @@
     head_sets = [[head * per_head + k for k in range(per_head)] for head in range(nf // per_head)]
 
     def gather_tokens(block):
-        part = lax.all_to_all(block, "fsdp", split_axis=1, concat_axis=0, tiled=True)
+        part = jnp.concatenate(
+            lax.all_to_all(
+                jnp.stack(jnp.split(block, lax.axis_size("fsdp"), axis=1)), "fsdp", 0, 0
+            ),
+            axis=0,
+        )
         part = lax.all_to_all(part, "sp", split_axis=0, concat_axis=1, tiled=True)
         return lax.all_gather(part, "fsdp", axis=0, tiled=True).reshape(tokens, width)
 

time: 1070 us -> 1030 us (0.963)
  other arithmetic: 151 us -> 133 us
  local copies, waits for them, and re-layouts: 79.8 us -> 63.4 us
    unnamed x6 -> x5, other arithmetic: 18.4 us -> 0.22 us
    unnamed x107 -> x112, local copies, waits for them, and re-layouts: 39.6 us -> 22.5 us
    convert_element_type x9 -> x8, other arithmetic: 45 us -> 44.9 us  [rounded(): lax.reduce_precision(array.astype(jnp.float32), 8, 7).astype(jnp.bfloat16)]
  transfers between devices with their start and end apart: 23 -> 23, of which waited for: 7 -> 7; matrix products, arithmetic and copies ran while one was open for 22% -> 21% of each run, Pallas kernels for 0% -> 0%
where the time goes in v1:
time: 1030 us; the launch traced here: 1020 us
  waiting for transfers between devices  276 us (27%)
  blocking collectives  254 us (25%)
  matrix products  170 us (17%)
  other arithmetic  133 us (13%)
  starting transfers between devices  112 us (11%)
  local copies, waits for them, and re-layouts  63.4 us (6%)
  between operations  15.2 us (1%)
    ppermute x4, waiting for transfers between devices, sum_over_line(): inward = lax.ppermute(partial, 'sp', [(0, 1), (3, 2)])  180 us
    psum x1, blocking collectives, per_device(): lax.psum((vectors, bias_out, bias_qkv, bias_up), 'sp')  127 us
    all_to_all x2, waiting for transfers between devices, scatter_tokens(): part = lax.all_to_all(part, 'sp', split_axis=1, concat_axis=0, tiled=True)  90.2 us
    all_to_all x2, starting transfers between devices, scatter_tokens(): part = lax.all_to_all(part, 'sp', split_axis=1, concat_axis=0, tiled=True)  68.4 us
    all_to_all x2, blocking collectives, gather_tokens(): part = lax.all_to_all(part, 'sp', split_axis=0, concat_axis=1, tiled=True)  58.7 us
    dot_general x4, matrix products, times_transposed(): lax.dot_general(former, latter, (((1,), (1,)), ((), ())), preferred_eleme...  51.7 us
    dot_general x4, matrix products, times(): return jnp.dot(former, latter, preferred_element_type=jnp.float32)  49.7 us
    convert_element_type x8, other arithmetic, rounded(): lax.reduce_precision(array.astype(jnp.float32), 8, 7).astype(jnp.bfloat16)  44.9 us
  transfers between devices with their start and end apart: 23, of which 7 were waited for; matrix products, arithmetic and copies ran while one was open for 21% of the time, Pallas kernels for 0%

profile of v1, /device:TPU:0, one launch (start us, length us, event | category | flops | bytes accessed | tf_op | source)
XLA Modules:
  0.0 1023.4 jit_solution(12187405230505349408)
XLA Ops:
  14.8 20.3 %all_to_all.132 = bf16[8,1,32,2048]{3,2,1,0:T(8,128)(2,1)S(1)} all-to-all(bf16[8,1,32,2048]{3,2,1,0:T(8,128)(2,1)S(1)} %bitcast_dynamic-update-slice_fusion.8), channel_id=1, replica_groups=mesh['fsdp'=8,'sp'=4] {'fsdp'}, dimensions={0} | all-to-all | bytes 2097152 | tf_op jit(solution)/shard_map/all_to_all | solution.py:186
  35.1 29.8 %all_to_all.133 = bf16[8,32,2048]{2,1,0:T(8,128)(2,1)S(1)} all-to-all(bf16[8,32,2048]{2,1,0:T(8,128)(2,1)S(1)} %bitcast.219), channel_id=1, replica_groups=mesh['fsdp'=8,'sp'=4] {'sp'}, dimensions={0} | all-to-all | bytes 2097152 | tf_op jit(solution)/shard_map/all_to_all | solution.py:191
  73.4 24.5 %all_to_all.134 = bf16[8,1,32,2048]{3,2,1,0:T(8,128)(2,1)S(1)} all-to-all(bf16[8,1,32,2048]{3,2,1,0:T(8,128)(2,1)S(1)} %bitcast_dynamic-update-slice_fusion), channel_id=1, replica_groups=mesh['fsdp'=8,'sp'=4] {'fsdp'}, dimensions={0} | all-to-all | bytes 2097152 | tf_op jit(solution)/shard_map/all_to_all | solution.py:186
  97.9 28.9 %all_to_all.135 = bf16[8,32,2048]{2,1,0:T(8,128)(2,1)S(1)} all-to-all(bf16[8,32,2048]{2,1,0:T(8,128)(2,1)S(1)} %bitcast.221), channel_id=1, replica_groups=mesh['fsdp'=8,'sp'=4] {'sp'}, dimensions={0} | all-to-all | bytes 2097152 | tf_op jit(solution)/shard_map/all_to_all | solution.py:191
  134.5 23.7 %all-gather = s32[8,1,1024]{2,1,0:T(1,128)S(1)} all-gather(s32[1,1,1024]{2,1,0:T(1,128)S(1)} %bitcast.250), channel_id=1, replica_groups=mesh['fsdp'=8,'sp'=4] {'fsdp'}, dimensions={0}, use_global_device_ids=true | all-gather | bytes 36864 | tf_op jit(solution)/shard_map/all_gather | solution.py:225
  261.9 15.3 %multiply_convert_fusion.1 = (bf16[2048,1024]{1,0:T(8,128)(2,1)}, f32[2048,1024]{1,0:T(8,128)}) fusion(f32[1024]{0:T(1024)S(1)} %dynamic_slice.14, bf16[2048,2048]{1,0:T(8,128)(2,1)} %get-tuple-element.26, bf16[1024,2048]{1,0:T(8,128)(2,1)S(1)} %copy-done.39), kind=kOutput, calls=%fused_computation.29 | convolution fusion | flops 8602517504 | bytes 25169920 | tf_op jit(solution)/shard_map/dot_general | solution.py:28
  277.3 17.5 %convert_reduce_fusion.2 = (f32[1024]{0:T(1024)}, bf16[2048,1024]{1,0:T(8,128)(2,1)}) fusion(f32[2048,1024]{1,0:T(8,128)} %get-tuple-element.60, f32[1024]{0:T(1024)S(1)} %dynamic_slice.14, bf16[2048,2048]{1,0:T(8,128)(2,1)S(1)} %bitcast.205, bf16[1024,2048]{1,0:T(8,128)(2,1)} %param.27), kind=kOutput, calls=%fused_computation.22 | convolution fusion | flops 8617196544 | bytes 25174016 | tf_op jit(solution)/shard_map/dot_general | solution.py:28
  294.8 14.1 %fusion.60 = f32[2048,2048]{1,0:T(8,128)} fusion(bf16[2048,1024]{1,0:T(8,128)(2,1)} %get-tuple-element.62, bf16[1024,2048]{1,0:T(8,128)(2,1)S(1)} %copy-done.39), kind=kOutput, calls=%fused_computation.162 | convolution fusion | flops 8589934592 | bytes 25165824 | tf_op jit(solution)/shard_map/dot_general | solution.py:34
  308.9 17.8 %multiply_reduce_fusion.1 = (f32[2048]{0:T(1024)S(1)}, f32[2048]{0:T(1024)S(1)}, f32[2048]{0:T(1024)S(1)}, f32[2048]{0:T(1024)S(1)}, bf16[2048,2048]{1,0:T(8,128)(2,1)}) fusion(bf16[16,128,2048]{2,1,0:T(8,128)(2,1)} %all-gather.4.cloned.1.call-done, f32[2048]{0:T(1024)S(1)} %get-tuple-element.48, f32[2048]{0:T(1024)S(1)} %get-tuple-element.49, ...), kind=kOutput, calls=%fused_computation.5 | convolution fusion | flops 6501163008 | bytes 39911424 | tf_op jit(solution)/shard_map/dot_general | solution.py:34
  327.9 8.2 fusion.31
  337.3 15.2 %reduce-precision_convert_fusion.7 = bf16[1024,2048]{1,0:T(8,128)(2,1)} fusion(bf16[2048,1024]{1,0:T(8,128)(2,1)} %get-tuple-element.62, bf16[2048,2048]{1,0:T(8,128)(2,1)} %get-tuple-element.26), kind=kOutput, calls=%fused_computation.25 | convolution fusion | flops 8594128896 | bytes 16777216 | tf_op jit(solution)/shard_map/dot_general | solution.py:22
  355.9 11.7 %fusion.59 = f32[2048,2048]{1,0:T(8,128)} fusion(bf16[2048,1024]{1,0:T(8,128)(2,1)S(1)} %copy-done.41, bf16[1024,2048]{1,0:T(8,128)(2,1)S(1)} %copy-done.40), kind=kOutput, calls=%fused_computation.161 | convolution fusion | flops 8589934592 | bytes 25165824 | tf_op jit(solution)/shard_map/dot_general | solution.py:34
  367.7 11.7 %reduce-precision_convert_fusion.1 = bf16[2048,2048]{1,0:T(8,128)(2,1)} fusion(f32[2048,2048]{1,0:T(8,128)} %fusion.59, bf16[2048,256]{1,0:T(8,128)(2,1)S(1)} %bitcast.228, bf16[2048,256]{1,0:T(8,128)(2,1)S(1)} %bitcast.227), kind=kOutput, calls=%fused_computation.7 | convolution fusion | flops 2160066560 | bytes 27262976 | tf_op jit(solution)/shard_map/dot_general | solution.py:28
  379.4 14.7 %reduce-precision_convert_fusion.4 = bf16[1024,2048]{1,0:T(8,128)(2,1)} fusion(bf16[2048,1024]{1,0:T(8,128)(2,1)} %get-tuple-element.59, bf16[2048,2048]{1,0:T(8,128)(2,1)} %bitcast.202), kind=kOutput, calls=%fused_computation.21 | convolution fusion | flops 8594128896 | bytes 16777216 | tf_op jit(solution)/shard_map/dot_general | solution.py:22
  403.7 8.3 reduce-precision_convert_fusion.10
  415.0 30.1 %collective-permute-done.6 = bf16[1024,2048]{1,0:T(8,128)(2,1)} collective-permute-done((bf16[1024,2048]{1,0:T(8,128)(2,1)}, bf16[1024,2048]{1,0:T(8,128)(2,1)}, u32[]{:S(2)}, u32[]{:S(2)}) %collective-permute-start.6) | collective-permute-done | bytes 4194336 | tf_op jit(solution)/shard_map/ppermute | solution.py:138
  445.1 7.8 reduce-precision_convert_fusion.6
  462.8 72.1 %collective-permute-done.9 = bf16[1024,2048]{1,0:T(8,128)(2,1)} collective-permute-done((bf16[1024,2048]{1,0:T(8,128)(2,1)}, bf16[1024,2048]{1,0:T(8,128)(2,1)}, u32[]{:S(2)}, u32[]{:S(2)}) %collective-permute-start.9) | collective-permute-done | bytes 4194336 | tf_op jit(solution)/shard_map/ppermute | solution.py:138
  545.5 56.5 %collective-permute-done = bf16[768,2048]{1,0:T(8,128)(2,1)} collective-permute-done((bf16[768,2048]{1,0:T(8,128)(2,1)}, bf16[768,2048]{1,0:T(8,128)(2,1)}, u32[]{:S(2)}, u32[]{:S(2)}) %collective-permute-start) | collective-permute-done | bytes 3145760 | tf_op jit(solution)/shard_map/ppermute | solution.py:138
  615.6 21.6 %collective-permute-done.3 = bf16[256,2048]{1,0:T(8,128)(2,1)S(1)} collective-permute-done((bf16[256,2048]{1,0:T(8,128)(2,1)S(1)}, bf16[256,2048]{1,0:T(8,128)(2,1)S(1)}, u32[]{:S(2)}, u32[]{:S(2)}) %collective-permute-start.3) | collective-permute-done | bytes 1048608 | tf_op jit(solution)/shard_map/ppermute | solution.py:138
  638.3 7.7 reduce-precision_convert_fusion.5
  658.0 64.0 %all-to-all-start.7 = ((bf16[2,128,2048]{2,0,1:T(2,128)(2,1)}), bf16[2,128,2048]{2,0,1:T(2,128)(2,1)}, u32[]{:S(2)}, u32[]{:S(2)}) async-start(bf16[2,128,2048]{2,0,1:T(2,128)(2,1)} %copy.188), calls=%async_computation.9 | async-start | bytes 2097152 | tf_op jit(solution)/shard_map/all_to_all | solution.py:197
  738.6 90.2 %all-to-all-done.7 = bf16[2,128,2048]{2,0,1:T(2,128)(2,1)} async-done(((bf16[2,128,2048]{2,0,1:T(2,128)(2,1)}), bf16[2,128,2048]{2,0,1:T(2,128)(2,1)}, u32[]{:S(2)}, u32[]{:S(2)}) %all-to-all-start.7) | async-done | bytes 1048608 | tf_op jit(solution)/shard_map/all_to_all | solution.py:197
  839.6 126.8 %all-reduce.1 = (f32[256,4]{0,1:T(4,128)S(1)}, f32[768]{0:T(1024)}, f32[256]{0:T(256)S(1)}, f32[1024]{0:T(1024)}) all-reduce(f32[256,4]{0,1:T(4,128)S(1)} %copy.203, f32[768]{0:T(1024)S(1)} %convert_reduce_fusion.3, f32[256]{0:T(256)S(1)} %dynamic_slice.15, f32[1024]{0:T(1024)S(1)} %copy-done.37), channel_id=1, replica_groups=mesh['fsdp'=8,'sp'=4] {'sp'}, use_global_device_ids=true, to_apply=%region_18.19 | all-reduce | flops 3072 | bytes 24576 | tf_op jit(solution)/shard_map/psum | solution.py:289
  (246 shorter events, 269.6 us)
Async XLA Ops:
  7.2 175.2 %copy-start = (bf16[768,2048]{1,0:T(8,128)(2,1)S(1)}, bf16[768,2048]{1,0:T(8,128)(2,1)}, u32[]{:S(2)}) copy-start(bf16[768,2048]{1,0:T(8,128)(2,1)} %param.21) | copy-start | bytes 9437188
  7.2 159.0 %all-gather.4.cloned.1.call-start = ((), (), s32[]{:S(2)}) async-start(), calls=%async_computation.13 | async-start | bytes 9437184 | tf_op jit(solution)/shard_map/all_gather | solution.py:192
  65.9 128.5 %all-gather.6.cloned.1.call-start = ((), (), s32[]{:S(2)}) async-start(), calls=%async_computation.15 | async-start | bytes 9437184 | tf_op jit(solution)/shard_map/all_gather | solution.py:192
  130.2 33.4 %all-to-all-start.2 = ((bf16[256,8,256]{0,2,1:T(8,128)(2,1)}), bf16[256,8,256]{0,2,1:T(8,128)(2,1)}, u32[]{:S(2)}, u32[]{:S(2)}) async-start(bf16[256,8,256]{0,2,1:T(8,128)(2,1)} %bitcast.218), calls=%async_computation.2 | async-start | bytes 2097152 | tf_op jit(solution)/shard_map/all_to_all | solution.py:227
  134.5 520.3 %reduce-scatter.8.cloned.1.call-start = ((), (), s32[]{:S(2)}) async-start(), calls=%async_computation.16 | async-start | bytes 9437184 | tf_op jit(solution)/shard_map/reduce_scatter | solution.py:196
  326.7 408.4 %reduce-scatter.6.cloned.1.call-start = ((), (), s32[]{:S(2)}) async-start(), calls=%async_computation.14 | async-start | bytes 9437184 | tf_op jit(solution)/shard_map/reduce_scatter | solution.py:196
  352.5 92.6 %collective-permute-start.6 = (bf16[1024,2048]{1,0:T(8,128)(2,1)}, bf16[1024,2048]{1,0:T(8,128)(2,1)}, u32[]{:S(2)}, u32[]{:S(2)}) collective-permute-start(bf16[1024,2048]{1,0:T(8,128)(2,1)} %reduce-precision_convert_fusion.7), channel_id=1, source_target_pairs={{0,1},{3,2},{4,5},{7,6},{8,9},{11,10},{12,13},{15,14},{16,17},{19,... | collective-permute-start | bytes 12582920 | tf_op jit(solution)/shard_map/ppermute | solution.py:138
  394.1 140.9 %collective-permute-start.9 = (bf16[1024,2048]{1,0:T(8,128)(2,1)}, bf16[1024,2048]{1,0:T(8,128)(2,1)}, u32[]{:S(2)}, u32[]{:S(2)}) collective-permute-start(bf16[1024,2048]{1,0:T(8,128)(2,1)} %reduce-precision_convert_fusion.4), channel_id=1, source_target_pairs={{0,1},{3,2},{4,5},{7,6},{8,9},{11,10},{12,13},{15,14},{16,17},{19,... | collective-permute-start | bytes 12582920 | tf_op jit(solution)/shard_map/ppermute | solution.py:138
  412.0 190.0 %collective-permute-start = (bf16[768,2048]{1,0:T(8,128)(2,1)}, bf16[768,2048]{1,0:T(8,128)(2,1)}, u32[]{:S(2)}, u32[]{:S(2)}) collective-permute-start(bf16[768,2048]{1,0:T(8,128)(2,1)} %reduce-precision_convert_fusion.10), channel_id=1, source_target_pairs={{0,1},{3,2},{4,5},{7,6},{8,9},{11,10},{12,13},{15,14},{16,17},{19,... | collective-permute-start | bytes 9437192 | tf_op jit(solution)/shard_map/ppermute | solution.py:138
  452.9 185.3 %collective-permute-start.7 = (bf16[1024,2048]{1,0:T(8,128)(2,1)}, bf16[1024,2048]{1,0:T(8,128)(2,1)}, u32[]{:S(2)}, u32[]{:S(2)}) collective-permute-start(bf16[1024,2048]{1,0:T(8,128)(2,1)} %reduce-precision_convert_fusion.6), channel_id=1, source_target_pairs={{1,2},{2,1},{5,6},{6,5},{9,10},{10,9},{13,14},{14,13},{17,18},{18,... | collective-permute-start | bytes 12582920 | tf_op jit(solution)/shard_map/ppermute | solution.py:140
  459.3 151.3 %all-to-all-start.9 = ((bf16[8,256,256]{2,1,0:T(8,128)(2,1)}), bf16[8,256,256]{2,1,0:T(8,128)(2,1)S(1)}, u32[]{:S(2)}, u32[]{:S(2)}) async-start(bf16[8,256,256]{2,1,0:T(8,128)(2,1)} %bitcast.84), calls=%async_computation.11 | async-start | bytes 2097152 | tf_op jit(solution)/shard_map/all_to_all | solution.py:275
  542.7 179.4 %collective-permute-start.10 = (bf16[1024,2048]{1,0:T(8,128)(2,1)}, bf16[1024,2048]{1,0:T(8,128)(2,1)}, u32[]{:S(2)}, u32[]{:S(2)}) collective-permute-start(bf16[1024,2048]{1,0:T(8,128)(2,1)} %reduce-precision_convert_fusion.3), channel_id=1, source_target_pairs={{1,2},{2,1},{5,6},{6,5},{9,10},{10,9},{13,14},{14,13},{17,18},{18,... | collective-permute-start | bytes 12582920 | tf_op jit(solution)/shard_map/ppermute | solution.py:140
  608.1 39.2 %collective-permute-start.1 = (bf16[768,2048]{1,0:T(8,128)(2,1)}, bf16[768,2048]{1,0:T(8,128)(2,1)}, u32[]{:S(2)}, u32[]{:S(2)}) collective-permute-start(bf16[768,2048]{1,0:T(8,128)(2,1)} %reduce-precision_convert_fusion.9), channel_id=1, source_target_pairs={{1,2},{2,1},{5,6},{6,5},{9,10},{10,9},{13,14},{14,13},{17,18},{18,... | collective-permute-start | bytes 9437192 | tf_op jit(solution)/shard_map/ppermute | solution.py:140
  610.8 26.3 %collective-permute-start.3 = (bf16[256,2048]{1,0:T(8,128)(2,1)S(1)}, bf16[256,2048]{1,0:T(8,128)(2,1)S(1)}, u32[]{:S(2)}, u32[]{:S(2)}) collective-permute-start(bf16[256,2048]{1,0:T(8,128)(2,1)S(1)} %bitcast.214), channel_id=1, source_target_pairs={{0,1},{3,2},{4,5},{7,6},{8,9},{11,10},{12,13},{15,14},{16,17},{19,... | collective-permute-start | bytes 3145736 | tf_op jit(solution)/shard_map/ppermute | solution.py:138
  637.5 93.5 %collective-permute-start.4 = (bf16[256,2048]{1,0:T(8,128)(2,1)S(1)}, bf16[256,2048]{1,0:T(8,128)(2,1)S(1)}, u32[]{:S(2)}, u32[]{:S(2)}) collective-permute-start(bf16[256,2048]{1,0:T(8,128)(2,1)S(1)} %reduce-precision_convert_fusion.12), channel_id=1, source_target_pairs={{1,2},{2,1},{5,6},{6,5},{9,10},{10,9},{13,14},{14,13},{17,18},{18,... | collective-permute-start | bytes 3145736 | tf_op jit(solution)/shard_map/ppermute | solution.py:140
  646.0 335.0 %collective-permute-start.8 = (bf16[1024,2048]{1,0:T(8,128)(2,1)}, bf16[1024,2048]{1,0:T(8,128)(2,1)}, u32[]{:S(2)}, u32[]{:S(2)}) collective-permute-start(bf16[1024,2048]{1,0:T(8,128)(2,1)} %reduce-precision_convert_fusion.5), channel_id=1, source_target_pairs={{1,0},{2,3},{5,4},{6,7},{9,8},{10,11},{13,12},{14,15},{17,16},{18,... | collective-permute-start | bytes 12582920 | tf_op jit(solution)/shard_map/ppermute | solution.py:142
  653.4 322.5 %collective-permute-start.2 = (bf16[768,2048]{1,0:T(8,128)(2,1)}, bf16[768,2048]{1,0:T(8,128)(2,1)}, u32[]{:S(2)}, u32[]{:S(2)}) collective-permute-start(bf16[768,2048]{1,0:T(8,128)(2,1)} %reduce-precision_convert_fusion.8), channel_id=1, source_target_pairs={{1,0},{2,3},{5,4},{6,7},{9,8},{10,11},{13,12},{14,15},{17,16},{18,... | collective-permute-start | bytes 9437192 | tf_op jit(solution)/shard_map/ppermute | solution.py:142
  658.0 170.7 %all-to-all-start.7 = ((bf16[2,128,2048]{2,0,1:T(2,128)(2,1)}), bf16[2,128,2048]{2,0,1:T(2,128)(2,1)}, u32[]{:S(2)}, u32[]{:S(2)}) async-start(bf16[2,128,2048]{2,0,1:T(2,128)(2,1)} %copy.188), calls=%async_computation.9 | async-start | bytes 2097152 | tf_op jit(solution)/shard_map/all_to_all | solution.py:197
  722.0 116.7 %reduce-scatter.10.cloned.1.call-start = ((), (), s32[]{:S(2)}) async-start(), calls=%async_computation.17 | async-start | bytes 1179648
  729.7 265.8 %collective-permute-start.11 = (bf16[1024,2048]{1,0:T(8,128)(2,1)}, bf16[1024,2048]{1,0:T(8,128)(2,1)}, u32[]{:S(2)}, u32[]{:S(2)}) collective-permute-start(bf16[1024,2048]{1,0:T(8,128)(2,1)} %reduce-precision_convert_fusion.2), channel_id=1, source_target_pairs={{1,0},{2,3},{5,4},{6,7},{9,8},{10,11},{13,12},{14,15},{17,16},{18,... | collective-permute-start | bytes 12582920 | tf_op jit(solution)/shard_map/ppermute | solution.py:142
  732.4 234.6 %collective-permute-start.5 = (bf16[256,2048]{1,0:T(8,128)(2,1)}, bf16[256,2048]{1,0:T(8,128)(2,1)}, u32[]{:S(2)}, u32[]{:S(2)}) collective-permute-start(bf16[256,2048]{1,0:T(8,128)(2,1)} %reduce-precision_convert_fusion.11), channel_id=1, source_target_pairs={{1,0},{2,3},{5,4},{6,7},{9,8},{10,11},{13,12},{14,15},{17,16},{18,... | collective-permute-start | bytes 3145736 | tf_op jit(solution)/shard_map/ppermute | solution.py:142
  828.8 143.6 %all-to-all-start.3 = ((bf16[2,128,2048]{2,0,1:T(2,128)(2,1)}), bf16[2,128,2048]{2,0,1:T(2,128)(2,1)}, u32[]{:S(2)}, u32[]{:S(2)}) async-start(bf16[2,128,2048]{2,0,1:T(2,128)(2,1)} %copy.173), calls=%async_computation.4 | async-start | bytes 2097152 | tf_op jit(solution)/shard_map/all_to_all | solution.py:197
  972.4 18.9 %all-to-all-start.8 = ((bf16[8,32,2048]{2,1,0:T(8,128)(2,1)}), bf16[8,32,2048]{2,1,0:T(8,128)(2,1)S(1)}, u32[]{:S(2)}, u32[]{:S(2)}) async-start(bf16[8,32,2048]{2,1,0:T(8,128)(2,1)} %bitcast.73), calls=%async_computation.10 | async-start | bytes 2097152 | tf_op jit(solution)/shard_map/all_to_all | solution.py:198
  991.3 19.7 %all-to-all-start.4 = ((bf16[8,32,2048]{2,1,0:T(8,128)(2,1)}), bf16[8,32,2048]{2,1,0:T(8,128)(2,1)}, u32[]{:S(2)}, u32[]{:S(2)}) async-start(bf16[8,32,2048]{2,1,0:T(8,128)(2,1)} %bitcast.36), calls=%async_computation.5 | async-start | bytes 2097152 | tf_op jit(solution)/shard_map/all_to_all | solution.py:198
  (45 other events, 701.9 us)
Sparse Core Ops, SparseCore 0:
  66.0 63.5 all-gather.3
  132.1 58.3 all-gather.5
  326.9 69.0 reduce-scatter.7
  400.2 78.0 reduce-scatter.5
  735.3 45.1 reduce-scatter.9
